TPU v7x, 32 devices: a whole 2x2x4 slice. The times are simulated.
32 devices in a mesh: groups: 2 (over x), win: 4 (over z), lat: 4 (over y, core).
Axes of the slice: x: 2, y: 2, z: 4, core: 2. Of those that a mesh axis runs over, the one named last changes fastest.
Arguments:
- thickness: float32 [8, 2, 3, 8, 64, 256], P(('groups', 'win'), None, None, None, 'lat'), parts along dimension 0, may hold values from 0.5 to 1.5
- obs_cells: int32 [8, 2, 1024], P(('groups', 'win'), None, 'lat'), parts along dimension 0, may hold values from 0 to 4095
- obs_values: float32 [8, 2, 1024], P(('groups', 'win'), None, 'lat'), parts along dimension 0, may hold values from -6 to 6
- ocean_mask: int32 [128, 256], P(('groups', 'lat')), parts along dimension 0, may hold values 0 or 1
- coupling: float32 [8, 8], replicated, may hold values from -1.2 to 1.2
- damping: float32 [8], replicated, may hold values from 0.05 to 0.8
Outputs:
- window_adjoint: float32 [8, 3, 8, 64, 256], P(('groups', 'win'), None, None, 'lat'), parts along dimension 0
- bias_gradient: float32 [16, 64, 256], P('groups', 'lat'), parts along dimension 0
There are 2 independent parts, one for each index of `groups`. A program takes and returns all parts, laid end to end along the dimension named above; an argument that names none is the same for every part. Nothing has to cross between parts.
Inputs may be any that keep to these rules, and one draw needn't show every extreme that they name: `obs_cells`: entry k of a step's list names a cell of the latitude block that starts at row (k // 256) * 16, as row * 256 + column within that block; a cell may be named several times.
All inputs are finite; a program needn't handle non-finite values. No bound on the sum of `ocean_mask` on one device may be relied on, other than what follows from the above.
Results may differ from a plain program's by a relative error of at most 0.00011.
Values sent between devices are 32-bit elements; how exact they have to be, the bound alone decides.
No kernel may reach another device: no remote copies, remote signals or barrier semaphores. Data moves between devices by JAX's collectives and lax.ppermute only.
A program may use at most 64 MiB of HBM per device.

v0:
```python
import jax
import jax.numpy as jnp
from jax import lax
from jax.sharding import PartitionSpec as P

STEP_DT = 0.2
THIRD = 1.0 / 3.0
TWO_THIRDS = 2.0 / 3.0


def with_halo(value, sides, width):
    for axis, dim in sides:
        count, length = (lax.axis_size(axis), value.shape[dim])
        up = [(i, (i + 1) % count) for i in range(count - 1)]
        down = [(j, i) for i, j in up]
        last = lax.slice_in_dim(value, length - width, length, axis=dim)
        initial = lax.slice_in_dim(value, 0, width, axis=dim)
        before = lax.ppermute(last, axis, up)
        after = lax.ppermute(initial, axis, down)
        value = jnp.concatenate([before, value, after], axis=dim)
    return value


def passed_along(value, axis, steps):
    count = lax.axis_size(axis)
    initial, last = (max(0, -steps), min(count, count - steps))
    return lax.ppermute(value, axis, [(source, source + steps) for source in range(initial, last)])


def tendency(state, ocean, fcor, edges, mix, rate):
    p_part = state[1]
    q_part = state[2]
    a_part = state[0]
    w_mid = edges[0][:, 1:-1]
    dxp = 0.5 * (jnp.roll(p_part, -1, axis=2) - jnp.roll(p_part, 1, axis=2))
    dyq = 0.5 * (edges[1][:, 2:] - edges[1][:, :-2])
    mixed = jnp.einsum("kl,krc->lrc", mix, dxp + dyq, precision=lax.Precision.HIGHEST)
    t_a = ocean * (mixed - rate * a_part)
    t_p = ocean * (
        0.5 * (jnp.roll(w_mid, -1, axis=2) - jnp.roll(w_mid, 1, axis=2))
        + fcor * q_part
        - rate * p_part
    )
    t_q = ocean * (0.5 * (edges[0][:, 2:] - edges[0][:, :-2]) - fcor * p_part - rate * q_part)
    return jnp.stack([t_a, t_p, t_q])


def runge_kutta(state, section_tend):
    first = state + STEP_DT * section_tend(state, 0)
    second = 0.75 * state + 0.25 * (first + STEP_DT * section_tend(first, 1))
    return THIRD * state + TWO_THIRDS * (second + STEP_DT * section_tend(second, 2))


def add_obs(state, cells, values):
    layer_a = state[0]
    flat = layer_a.reshape(layer_a.shape[0], -1).at[:, cells].add(values[None, :])
    return state.at[0].set(flat.reshape(layer_a.shape))


def per_device(thickness, obs_cells, obs_values, ocean_mask, coupling, damping):
    rows = ocean_mask.shape[0]
    total_rows = rows * lax.axis_size("lat")
    first_row = lax.axis_index("lat") * rows
    mix = jnp.eye(coupling.shape[0], dtype=jnp.float32) + coupling
    rate = damping[:, None, None]
    steps = thickness.shape[1]
    ocean = ocean_mask.astype(jnp.float32)
    global_rows = first_row + jnp.arange(rows, dtype=jnp.int32)
    fcor = (0.3 + 0.4 * (global_rows.astype(jnp.float32) / total_rows - 0.5))[:, None]

    def adjoint_step(state, thick):

        def section_tend(current, section):
            pair = jnp.stack([thick[section] * current[0], current[2]])
            edges = with_halo(pair, (("lat", 2),), 1)
            return tendency(current, ocean, fcor, edges, mix, rate)

        return runge_kutta(state, section_tend)

    def integrate(state):
        bias = jnp.zeros(state.shape[1:], jnp.float32)
        for step in reversed(range(steps)):
            state = add_obs(state, obs_cells[0, step], obs_values[0, step])
            state = adjoint_step(state, thickness[0, step])
            bias = bias + STEP_DT * state[0]
        return (state, bias)

    zero_state = jnp.zeros((3,) + thickness.shape[3:], jnp.float32)
    rounds = lax.axis_size("win") - 1

    def relay_round(index, carry):
        start_state, unused = integrate(carry)
        return passed_along(start_state, "win", -1)

    incoming = lax.fori_loop(0, rounds, relay_round, zero_state)
    lam, bias = integrate(incoming)
    total_bias = lax.psum(bias, "win")
    return (lam[None], total_bias)


def solution(mesh):
    in_specs = (
        P(("groups", "win"), None, None, None, "lat", None),
        P(("groups", "win"), None, "lat"),
        P(("groups", "win"), None, "lat"),
        P(("groups", "lat"), None),
        P(),
        P(),
    )
    out_specs = (P(("groups", "win"), None, None, "lat", None), P("groups", "lat", None))
    return jax.shard_map(
        per_device, mesh=mesh, in_specs=in_specs, out_specs=out_specs, check_vma=False
    )
```

profile of v0, /device:TPU:0, one launch (start us, length us, event | category | flops | bytes accessed | tf_op | source)
XLA Modules:
  0.0 356.3 jit_solution(15236490072825664713)
XLA Ops:
  13.6 232.1 %while.17 = (s32[]{:T(128)}, f32[3,8,16,256]{3,1,2,0:T(8,128)S(1)}, s32[1,2,256]{2,1,0:T(2,128)}, f32[1,2,256]{2,1,0:T(2,128)}, f32[16,256]{1,0:T(8,128)S(1)}, /...) while((s32[]{:T(128)}, f32[3,8,16,256]{3,1,2,0:T(8,128)S(1)}, ...), condition=%wide.region_3.4_spmd.clone, body=%wide.region_0.3_spmd.clone.sunk | while | flops 31856224 | bytes 54825772 | solution.py:95
  31.4 4.5 %collective-permute-start.3 = (f32[2,8,1,256]{3,1,2,0:T(8,128)S(1)}, f32[2,8,1,256]{3,1,2,0:T(8,128)S(1)}, u32[]{:S(2)}, u32[]{:S(2)}) collective-permute-start(f32[2,8,1,256]{3,1,2,0:T(8,128)S(1)} %get-tuple-element.601), channel_id=1, source_target_pairs={{0,1},{1,2},{2,3},{4,5},{5,6},{6,7},{8,9},{9,10},{10,11},{12,13},{... | collective-permute-start | bytes 49160 | tf_op jit(solution)/shard_map/while/body/eval_jaxpr/ppermute | solution.py:18
  39.8 4.3 %collective-permute-start.5 = (f32[2,8,1,256]{3,1,2,0:T(8,128)S(1)}, f32[2,8,1,256]{3,1,2,0:T(8,128)S(1)}, u32[]{:S(2)}, u32[]{:S(2)}) collective-permute-start(f32[2,8,1,256]{3,1,2,0:T(8,128)S(1)} %get-tuple-element.617), channel_id=1, source_target_pairs={{0,1},{1,2},{2,3},{4,5},{5,6},{6,7},{8,9},{9,10},{10,11},{12,13},{... | collective-permute-start | bytes 49160 | tf_op jit(solution)/shard_map/while/body/eval_jaxpr/ppermute | solution.py:18
  53.1 4.9 %collective-permute-start.7 = (f32[2,8,1,256]{3,1,2,0:T(8,128)S(1)}, f32[2,8,1,256]{3,1,2,0:T(8,128)S(1)}, u32[]{:S(2)}, u32[]{:S(2)}) collective-permute-start(f32[2,8,1,256]{3,1,2,0:T(8,128)S(1)} %get-tuple-element.635), channel_id=1, source_target_pairs={{0,1},{1,2},{2,3},{4,5},{5,6},{6,7},{8,9},{9,10},{10,11},{12,13},{... | collective-permute-start | bytes 49160 | tf_op jit(solution)/shard_map/while/body/eval_jaxpr/ppermute | solution.py:18
  62.0 4.9 %collective-permute-start.9 = (f32[2,8,1,256]{3,1,2,0:T(8,128)S(1)}, f32[2,8,1,256]{3,1,2,0:T(8,128)S(1)}, u32[]{:S(2)}, u32[]{:S(2)}) collective-permute-start(f32[2,8,1,256]{3,1,2,0:T(8,128)S(1)} %get-tuple-element.651), channel_id=1, source_target_pairs={{0,1},{1,2},{2,3},{4,5},{5,6},{6,7},{8,9},{9,10},{10,11},{12,13},{... | collective-permute-start | bytes 49160 | tf_op jit(solution)/shard_map/while/body/eval_jaxpr/ppermute | solution.py:18
  70.8 4.9 %collective-permute-start.11 = (f32[2,8,1,256]{3,1,2,0:T(8,128)S(1)}, f32[2,8,1,256]{3,1,2,0:T(8,128)S(1)}, u32[]{:S(2)}, u32[]{:S(2)}) collective-permute-start(f32[2,8,1,256]{3,1,2,0:T(8,128)S(1)} %get-tuple-element.667), channel_id=1, source_target_pairs={{0,1},{1,2},{2,3},{4,5},{5,6},{6,7},{8,9},{9,10},{10,11},{12,13},{... | collective-permute-start | bytes 49160 | tf_op jit(solution)/shard_map/while/body/eval_jaxpr/ppermute | solution.py:18
  79.5 11.2 %collective-permute-done.12 = f32[3,8,16,256]{3,1,2,0:T(8,128)S(1)} collective-permute-done((f32[3,8,16,256]{3,1,2,0:T(8,128)S(1)}, f32[3,8,16,256]{3,1,2,0:T(8,128)S(1)}, u32[]{:S(2)}, u32[]{:S(2)}) %collective-permute-start.12) | collective-permute-done | bytes 393248 | tf_op jit(solution)/shard_map/while/body/eval_jaxpr/ppermute | solution.py:27
  99.2 4.4 %collective-permute-start.1 = (f32[2,8,1,256]{3,1,2,0:T(8,128)}, f32[2,8,1,256]{3,1,2,0:T(8,128)}, u32[]{:S(2)}, u32[]{:S(2)}) collective-permute-start(f32[2,8,1,256]{3,1,2,0:T(8,128)} %get-tuple-element.585), channel_id=1, source_target_pairs={{0,1},{1,2},{2,3},{4,5},{5,6},{6,7},{8,9},{9,10},{10,11},{12,13},{... | collective-permute-start | bytes 49160 | tf_op jit(solution)/shard_map/while/body/eval_jaxpr/ppermute | solution.py:18
  109.1 4.3 %collective-permute-start.3 = (f32[2,8,1,256]{3,1,2,0:T(8,128)S(1)}, f32[2,8,1,256]{3,1,2,0:T(8,128)S(1)}, u32[]{:S(2)}, u32[]{:S(2)}) collective-permute-start(f32[2,8,1,256]{3,1,2,0:T(8,128)S(1)} %get-tuple-element.601), channel_id=1, source_target_pairs={{0,1},{1,2},{2,3},{4,5},{5,6},{6,7},{8,9},{9,10},{10,11},{12,13},{... | collective-permute-start | bytes 49160 | tf_op jit(solution)/shard_map/while/body/eval_jaxpr/ppermute | solution.py:18
  117.3 4.3 %collective-permute-start.5 = (f32[2,8,1,256]{3,1,2,0:T(8,128)S(1)}, f32[2,8,1,256]{3,1,2,0:T(8,128)S(1)}, u32[]{:S(2)}, u32[]{:S(2)}) collective-permute-start(f32[2,8,1,256]{3,1,2,0:T(8,128)S(1)} %get-tuple-element.617), channel_id=1, source_target_pairs={{0,1},{1,2},{2,3},{4,5},{5,6},{6,7},{8,9},{9,10},{10,11},{12,13},{... | collective-permute-start | bytes 49160 | tf_op jit(solution)/shard_map/while/body/eval_jaxpr/ppermute | solution.py:18
  130.6 4.9 %collective-permute-start.7 = (f32[2,8,1,256]{3,1,2,0:T(8,128)S(1)}, f32[2,8,1,256]{3,1,2,0:T(8,128)S(1)}, u32[]{:S(2)}, u32[]{:S(2)}) collective-permute-start(f32[2,8,1,256]{3,1,2,0:T(8,128)S(1)} %get-tuple-element.635), channel_id=1, source_target_pairs={{0,1},{1,2},{2,3},{4,5},{5,6},{6,7},{8,9},{9,10},{10,11},{12,13},{... | collective-permute-start | bytes 49160 | tf_op jit(solution)/shard_map/while/body/eval_jaxpr/ppermute | solution.py:18
  139.6 4.9 %collective-permute-start.9 = (f32[2,8,1,256]{3,1,2,0:T(8,128)S(1)}, f32[2,8,1,256]{3,1,2,0:T(8,128)S(1)}, u32[]{:S(2)}, u32[]{:S(2)}) collective-permute-start(f32[2,8,1,256]{3,1,2,0:T(8,128)S(1)} %get-tuple-element.651), channel_id=1, source_target_pairs={{0,1},{1,2},{2,3},{4,5},{5,6},{6,7},{8,9},{9,10},{10,11},{12,13},{... | collective-permute-start | bytes 49160 | tf_op jit(solution)/shard_map/while/body/eval_jaxpr/ppermute | solution.py:18
  148.3 4.9 %collective-permute-start.11 = (f32[2,8,1,256]{3,1,2,0:T(8,128)S(1)}, f32[2,8,1,256]{3,1,2,0:T(8,128)S(1)}, u32[]{:S(2)}, u32[]{:S(2)}) collective-permute-start(f32[2,8,1,256]{3,1,2,0:T(8,128)S(1)} %get-tuple-element.667), channel_id=1, source_target_pairs={{0,1},{1,2},{2,3},{4,5},{5,6},{6,7},{8,9},{9,10},{10,11},{12,13},{... | collective-permute-start | bytes 49160 | tf_op jit(solution)/shard_map/while/body/eval_jaxpr/ppermute | solution.py:18
  157.0 11.2 %collective-permute-done.12 = f32[3,8,16,256]{3,1,2,0:T(8,128)S(1)} collective-permute-done((f32[3,8,16,256]{3,1,2,0:T(8,128)S(1)}, f32[3,8,16,256]{3,1,2,0:T(8,128)S(1)}, u32[]{:S(2)}, u32[]{:S(2)}) %collective-permute-start.12) | collective-permute-done | bytes 393248 | tf_op jit(solution)/shard_map/while/body/eval_jaxpr/ppermute | solution.py:27
  176.7 4.4 %collective-permute-start.1 = (f32[2,8,1,256]{3,1,2,0:T(8,128)}, f32[2,8,1,256]{3,1,2,0:T(8,128)}, u32[]{:S(2)}, u32[]{:S(2)}) collective-permute-start(f32[2,8,1,256]{3,1,2,0:T(8,128)} %get-tuple-element.585), channel_id=1, source_target_pairs={{0,1},{1,2},{2,3},{4,5},{5,6},{6,7},{8,9},{9,10},{10,11},{12,13},{... | collective-permute-start | bytes 49160 | tf_op jit(solution)/shard_map/while/body/eval_jaxpr/ppermute | solution.py:18
  186.7 4.3 %collective-permute-start.3 = (f32[2,8,1,256]{3,1,2,0:T(8,128)S(1)}, f32[2,8,1,256]{3,1,2,0:T(8,128)S(1)}, u32[]{:S(2)}, u32[]{:S(2)}) collective-permute-start(f32[2,8,1,256]{3,1,2,0:T(8,128)S(1)} %get-tuple-element.601), channel_id=1, source_target_pairs={{0,1},{1,2},{2,3},{4,5},{5,6},{6,7},{8,9},{9,10},{10,11},{12,13},{... | collective-permute-start | bytes 49160 | tf_op jit(solution)/shard_map/while/body/eval_jaxpr/ppermute | solution.py:18
  194.8 4.3 %collective-permute-start.5 = (f32[2,8,1,256]{3,1,2,0:T(8,128)S(1)}, f32[2,8,1,256]{3,1,2,0:T(8,128)S(1)}, u32[]{:S(2)}, u32[]{:S(2)}) collective-permute-start(f32[2,8,1,256]{3,1,2,0:T(8,128)S(1)} %get-tuple-element.617), channel_id=1, source_target_pairs={{0,1},{1,2},{2,3},{4,5},{5,6},{6,7},{8,9},{9,10},{10,11},{12,13},{... | collective-permute-start | bytes 49160 | tf_op jit(solution)/shard_map/while/body/eval_jaxpr/ppermute | solution.py:18
  208.1 4.9 %collective-permute-start.7 = (f32[2,8,1,256]{3,1,2,0:T(8,128)S(1)}, f32[2,8,1,256]{3,1,2,0:T(8,128)S(1)}, u32[]{:S(2)}, u32[]{:S(2)}) collective-permute-start(f32[2,8,1,256]{3,1,2,0:T(8,128)S(1)} %get-tuple-element.635), channel_id=1, source_target_pairs={{0,1},{1,2},{2,3},{4,5},{5,6},{6,7},{8,9},{9,10},{10,11},{12,13},{... | collective-permute-start | bytes 49160 | tf_op jit(solution)/shard_map/while/body/eval_jaxpr/ppermute | solution.py:18
  217.1 4.9 %collective-permute-start.9 = (f32[2,8,1,256]{3,1,2,0:T(8,128)S(1)}, f32[2,8,1,256]{3,1,2,0:T(8,128)S(1)}, u32[]{:S(2)}, u32[]{:S(2)}) collective-permute-start(f32[2,8,1,256]{3,1,2,0:T(8,128)S(1)} %get-tuple-element.651), channel_id=1, source_target_pairs={{0,1},{1,2},{2,3},{4,5},{5,6},{6,7},{8,9},{9,10},{10,11},{12,13},{... | collective-permute-start | bytes 49160 | tf_op jit(solution)/shard_map/while/body/eval_jaxpr/ppermute | solution.py:18
  225.8 4.9 %collective-permute-start.11 = (f32[2,8,1,256]{3,1,2,0:T(8,128)S(1)}, f32[2,8,1,256]{3,1,2,0:T(8,128)S(1)}, u32[]{:S(2)}, u32[]{:S(2)}) collective-permute-start(f32[2,8,1,256]{3,1,2,0:T(8,128)S(1)} %get-tuple-element.667), channel_id=1, source_target_pairs={{0,1},{1,2},{2,3},{4,5},{5,6},{6,7},{8,9},{9,10},{10,11},{12,13},{... | collective-permute-start | bytes 49160 | tf_op jit(solution)/shard_map/while/body/eval_jaxpr/ppermute | solution.py:18
  234.5 11.2 %collective-permute-done.12 = f32[3,8,16,256]{3,1,2,0:T(8,128)S(1)} collective-permute-done((f32[3,8,16,256]{3,1,2,0:T(8,128)S(1)}, f32[3,8,16,256]{3,1,2,0:T(8,128)S(1)}, u32[]{:S(2)}, u32[]{:S(2)}) %collective-permute-start.12) | collective-permute-done | bytes 393248 | tf_op jit(solution)/shard_map/while/body/eval_jaxpr/ppermute | solution.py:27
  260.8 4.4 %collective-permute-start.15 = (f32[2,8,1,256]{3,1,2,0:T(8,128)S(1)}, f32[2,8,1,256]{3,1,2,0:T(8,128)S(1)}, u32[]{:S(2)}, u32[]{:S(2)}) collective-permute-start(f32[2,8,1,256]{3,1,2,0:T(8,128)S(1)} %get-tuple-element.365), channel_id=1, source_target_pairs={{0,1},{1,2},{2,3},{4,5},{5,6},{6,7},{8,9},{9,10},{10,11},{12,13},{... | collective-permute-start | bytes 49160 | tf_op jit(solution)/shard_map/ppermute | solution.py:18
  293.9 3.9 %collective-permute-start.21 = (f32[2,8,1,256]{3,1,2,0:T(8,128)S(1)}, f32[2,8,1,256]{3,1,2,0:T(8,128)S(1)}, u32[]{:S(2)}, u32[]{:S(2)}) collective-permute-start(f32[2,8,1,256]{3,1,2,0:T(8,128)S(1)} %get-tuple-element.359), channel_id=1, source_target_pairs={{0,1},{1,2},{2,3},{4,5},{5,6},{6,7},{8,9},{9,10},{10,11},{12,13},{... | collective-permute-start | bytes 49160 | tf_op jit(solution)/shard_map/ppermute | solution.py:18
  313.3 34.5 %all-reduce.2.cloned.1.call-done = f32[8,16,256]{2,0,1:T(8,128)} async-done(((f32[8,16,256]{2,0,1:T(8,128)}), f32[8,16,256]{2,0,1:T(8,128)}) %all-reduce.2.cloned.1.call-update) | async-done | bytes 131088 | tf_op jit(solution)/shard_map/psum | solution.py:97
  (617 shorter events, 184.2 us)
Async XLA Ops:
  7.2 340.7 %all-reduce.2.cloned.1.call-start = ((), (), s32[]{:S(2)}) async-start(), calls=%async_computation | async-start | bytes 262144 | tf_op jit(solution)/shard_map/psum | solution.py:97
  20.9 6.7 %collective-permute-start = (f32[2,8,1,256]{3,1,2,0:T(8,128)}, f32[2,8,1,256]{3,1,2,0:T(8,128)}, u32[]{:S(2)}, u32[]{:S(2)}) collective-permute-start(f32[2,8,1,256]{3,1,2,0:T(8,128)} %get-tuple-element.584), channel_id=1, source_target_pairs={{1,0},{2,1},{3,2},{5,4},{6,5},{7,6},{9,8},{10,9},{11,10},{13,12},{... | collective-permute-start | bytes 49160 | tf_op jit(solution)/shard_map/while/body/eval_jaxpr/ppermute | solution.py:19
  30.1 5.8 %collective-permute-start.2 = (f32[2,8,1,256]{3,1,2,0:T(8,128)S(1)}, f32[2,8,1,256]{3,1,2,0:T(8,128)S(1)}, u32[]{:S(2)}, u32[]{:S(2)}) collective-permute-start(f32[2,8,1,256]{3,1,2,0:T(8,128)S(1)} %get-tuple-element.600), channel_id=1, source_target_pairs={{1,0},{2,1},{3,2},{5,4},{6,5},{7,6},{9,8},{10,9},{11,10},{13,12},{... | collective-permute-start | bytes 49160 | tf_op jit(solution)/shard_map/while/body/eval_jaxpr/ppermute | solution.py:19
  51.8 6.8 %collective-permute-start.6 = (f32[2,8,1,256]{3,1,2,0:T(8,128)S(1)}, f32[2,8,1,256]{3,1,2,0:T(8,128)S(1)}, u32[]{:S(2)}, u32[]{:S(2)}) collective-permute-start(f32[2,8,1,256]{3,1,2,0:T(8,128)S(1)} %get-tuple-element.634), channel_id=1, source_target_pairs={{1,0},{2,1},{3,2},{5,4},{6,5},{7,6},{9,8},{10,9},{11,10},{13,12},{... | collective-permute-start | bytes 49160 | tf_op jit(solution)/shard_map/while/body/eval_jaxpr/ppermute | solution.py:19
  53.1 5.7 %collective-permute-start.7 = (f32[2,8,1,256]{3,1,2,0:T(8,128)S(1)}, f32[2,8,1,256]{3,1,2,0:T(8,128)S(1)}, u32[]{:S(2)}, u32[]{:S(2)}) collective-permute-start(f32[2,8,1,256]{3,1,2,0:T(8,128)S(1)} %get-tuple-element.635), channel_id=1, source_target_pairs={{0,1},{1,2},{2,3},{4,5},{5,6},{6,7},{8,9},{9,10},{10,11},{12,13},{... | collective-permute-start | bytes 49160 | tf_op jit(solution)/shard_map/while/body/eval_jaxpr/ppermute | solution.py:18
  60.7 6.2 %collective-permute-start.8 = (f32[2,8,1,256]{3,1,2,0:T(8,128)S(1)}, f32[2,8,1,256]{3,1,2,0:T(8,128)S(1)}, u32[]{:S(2)}, u32[]{:S(2)}) collective-permute-start(f32[2,8,1,256]{3,1,2,0:T(8,128)S(1)} %get-tuple-element.650), channel_id=1, source_target_pairs={{1,0},{2,1},{3,2},{5,4},{6,5},{7,6},{9,8},{10,9},{11,10},{13,12},{... | collective-permute-start | bytes 49160 | tf_op jit(solution)/shard_map/while/body/eval_jaxpr/ppermute | solution.py:19
  62.0 5.7 %collective-permute-start.9 = (f32[2,8,1,256]{3,1,2,0:T(8,128)S(1)}, f32[2,8,1,256]{3,1,2,0:T(8,128)S(1)}, u32[]{:S(2)}, u32[]{:S(2)}) collective-permute-start(f32[2,8,1,256]{3,1,2,0:T(8,128)S(1)} %get-tuple-element.651), channel_id=1, source_target_pairs={{0,1},{1,2},{2,3},{4,5},{5,6},{6,7},{8,9},{9,10},{10,11},{12,13},{... | collective-permute-start | bytes 49160 | tf_op jit(solution)/shard_map/while/body/eval_jaxpr/ppermute | solution.py:18
  69.5 6.2 %collective-permute-start.10 = (f32[2,8,1,256]{3,1,2,0:T(8,128)S(1)}, f32[2,8,1,256]{3,1,2,0:T(8,128)S(1)}, u32[]{:S(2)}, u32[]{:S(2)}) collective-permute-start(f32[2,8,1,256]{3,1,2,0:T(8,128)S(1)} %get-tuple-element.666), channel_id=1, source_target_pairs={{1,0},{2,1},{3,2},{5,4},{6,5},{7,6},{9,8},{10,9},{11,10},{13,12},{... | collective-permute-start | bytes 49160 | tf_op jit(solution)/shard_map/while/body/eval_jaxpr/ppermute | solution.py:19
  78.2 12.5 %collective-permute-start.12 = (f32[3,8,16,256]{3,1,2,0:T(8,128)S(1)}, f32[3,8,16,256]{3,1,2,0:T(8,128)S(1)}, u32[]{:S(2)}, u32[]{:S(2)}) collective-permute-start(f32[3,8,16,256]{3,1,2,0:T(8,128)S(1)} %fusion.480), channel_id=1, source_target_pairs={{4,0},{8,4},{12,8},{5,1},{9,5},{13,9},{6,2},{10,6},{14,10},{7,3},{... | collective-permute-start | bytes 1179656 | tf_op jit(solution)/shard_map/while/body/eval_jaxpr/ppermute | solution.py:27
  97.9 7.4 %collective-permute-start = (f32[2,8,1,256]{3,1,2,0:T(8,128)}, f32[2,8,1,256]{3,1,2,0:T(8,128)}, u32[]{:S(2)}, u32[]{:S(2)}) collective-permute-start(f32[2,8,1,256]{3,1,2,0:T(8,128)} %get-tuple-element.584), channel_id=1, source_target_pairs={{1,0},{2,1},{3,2},{5,4},{6,5},{7,6},{9,8},{10,9},{11,10},{13,12},{... | collective-permute-start | bytes 49160 | tf_op jit(solution)/shard_map/while/body/eval_jaxpr/ppermute | solution.py:19
  99.2 6.1 %collective-permute-start.1 = (f32[2,8,1,256]{3,1,2,0:T(8,128)}, f32[2,8,1,256]{3,1,2,0:T(8,128)}, u32[]{:S(2)}, u32[]{:S(2)}) collective-permute-start(f32[2,8,1,256]{3,1,2,0:T(8,128)} %get-tuple-element.585), channel_id=1, source_target_pairs={{0,1},{1,2},{2,3},{4,5},{5,6},{6,7},{8,9},{9,10},{10,11},{12,13},{... | collective-permute-start | bytes 49160 | tf_op jit(solution)/shard_map/while/body/eval_jaxpr/ppermute | solution.py:18
  129.3 6.8 %collective-permute-start.6 = (f32[2,8,1,256]{3,1,2,0:T(8,128)S(1)}, f32[2,8,1,256]{3,1,2,0:T(8,128)S(1)}, u32[]{:S(2)}, u32[]{:S(2)}) collective-permute-start(f32[2,8,1,256]{3,1,2,0:T(8,128)S(1)} %get-tuple-element.634), channel_id=1, source_target_pairs={{1,0},{2,1},{3,2},{5,4},{6,5},{7,6},{9,8},{10,9},{11,10},{13,12},{... | collective-permute-start | bytes 49160 | tf_op jit(solution)/shard_map/while/body/eval_jaxpr/ppermute | solution.py:19
  138.3 6.2 %collective-permute-start.8 = (f32[2,8,1,256]{3,1,2,0:T(8,128)S(1)}, f32[2,8,1,256]{3,1,2,0:T(8,128)S(1)}, u32[]{:S(2)}, u32[]{:S(2)}) collective-permute-start(f32[2,8,1,256]{3,1,2,0:T(8,128)S(1)} %get-tuple-element.650), channel_id=1, source_target_pairs={{1,0},{2,1},{3,2},{5,4},{6,5},{7,6},{9,8},{10,9},{11,10},{13,12},{... | collective-permute-start | bytes 49160 | tf_op jit(solution)/shard_map/while/body/eval_jaxpr/ppermute | solution.py:19
  147.0 6.2 %collective-permute-start.10 = (f32[2,8,1,256]{3,1,2,0:T(8,128)S(1)}, f32[2,8,1,256]{3,1,2,0:T(8,128)S(1)}, u32[]{:S(2)}, u32[]{:S(2)}) collective-permute-start(f32[2,8,1,256]{3,1,2,0:T(8,128)S(1)} %get-tuple-element.666), channel_id=1, source_target_pairs={{1,0},{2,1},{3,2},{5,4},{6,5},{7,6},{9,8},{10,9},{11,10},{13,12},{... | collective-permute-start | bytes 49160 | tf_op jit(solution)/shard_map/while/body/eval_jaxpr/ppermute | solution.py:19
  155.7 12.5 %collective-permute-start.12 = (f32[3,8,16,256]{3,1,2,0:T(8,128)S(1)}, f32[3,8,16,256]{3,1,2,0:T(8,128)S(1)}, u32[]{:S(2)}, u32[]{:S(2)}) collective-permute-start(f32[3,8,16,256]{3,1,2,0:T(8,128)S(1)} %fusion.480), channel_id=1, source_target_pairs={{4,0},{8,4},{12,8},{5,1},{9,5},{13,9},{6,2},{10,6},{14,10},{7,3},{... | collective-permute-start | bytes 1179656 | tf_op jit(solution)/shard_map/while/body/eval_jaxpr/ppermute | solution.py:27
  175.5 7.4 %collective-permute-start = (f32[2,8,1,256]{3,1,2,0:T(8,128)}, f32[2,8,1,256]{3,1,2,0:T(8,128)}, u32[]{:S(2)}, u32[]{:S(2)}) collective-permute-start(f32[2,8,1,256]{3,1,2,0:T(8,128)} %get-tuple-element.584), channel_id=1, source_target_pairs={{1,0},{2,1},{3,2},{5,4},{6,5},{7,6},{9,8},{10,9},{11,10},{13,12},{... | collective-permute-start | bytes 49160 | tf_op jit(solution)/shard_map/while/body/eval_jaxpr/ppermute | solution.py:19
  176.7 6.1 %collective-permute-start.1 = (f32[2,8,1,256]{3,1,2,0:T(8,128)}, f32[2,8,1,256]{3,1,2,0:T(8,128)}, u32[]{:S(2)}, u32[]{:S(2)}) collective-permute-start(f32[2,8,1,256]{3,1,2,0:T(8,128)} %get-tuple-element.585), channel_id=1, source_target_pairs={{0,1},{1,2},{2,3},{4,5},{5,6},{6,7},{8,9},{9,10},{10,11},{12,13},{... | collective-permute-start | bytes 49160 | tf_op jit(solution)/shard_map/while/body/eval_jaxpr/ppermute | solution.py:18
  206.8 6.8 %collective-permute-start.6 = (f32[2,8,1,256]{3,1,2,0:T(8,128)S(1)}, f32[2,8,1,256]{3,1,2,0:T(8,128)S(1)}, u32[]{:S(2)}, u32[]{:S(2)}) collective-permute-start(f32[2,8,1,256]{3,1,2,0:T(8,128)S(1)} %get-tuple-element.634), channel_id=1, source_target_pairs={{1,0},{2,1},{3,2},{5,4},{6,5},{7,6},{9,8},{10,9},{11,10},{13,12},{... | collective-permute-start | bytes 49160 | tf_op jit(solution)/shard_map/while/body/eval_jaxpr/ppermute | solution.py:19
  215.8 6.2 %collective-permute-start.8 = (f32[2,8,1,256]{3,1,2,0:T(8,128)S(1)}, f32[2,8,1,256]{3,1,2,0:T(8,128)S(1)}, u32[]{:S(2)}, u32[]{:S(2)}) collective-permute-start(f32[2,8,1,256]{3,1,2,0:T(8,128)S(1)} %get-tuple-element.650), channel_id=1, source_target_pairs={{1,0},{2,1},{3,2},{5,4},{6,5},{7,6},{9,8},{10,9},{11,10},{13,12},{... | collective-permute-start | bytes 49160 | tf_op jit(solution)/shard_map/while/body/eval_jaxpr/ppermute | solution.py:19
  224.5 6.2 %collective-permute-start.10 = (f32[2,8,1,256]{3,1,2,0:T(8,128)S(1)}, f32[2,8,1,256]{3,1,2,0:T(8,128)S(1)}, u32[]{:S(2)}, u32[]{:S(2)}) collective-permute-start(f32[2,8,1,256]{3,1,2,0:T(8,128)S(1)} %get-tuple-element.666), channel_id=1, source_target_pairs={{1,0},{2,1},{3,2},{5,4},{6,5},{7,6},{9,8},{10,9},{11,10},{13,12},{... | collective-permute-start | bytes 49160 | tf_op jit(solution)/shard_map/while/body/eval_jaxpr/ppermute | solution.py:19
  233.2 12.5 %collective-permute-start.12 = (f32[3,8,16,256]{3,1,2,0:T(8,128)S(1)}, f32[3,8,16,256]{3,1,2,0:T(8,128)S(1)}, u32[]{:S(2)}, u32[]{:S(2)}) collective-permute-start(f32[3,8,16,256]{3,1,2,0:T(8,128)S(1)} %fusion.480), channel_id=1, source_target_pairs={{4,0},{8,4},{12,8},{5,1},{9,5},{13,9},{6,2},{10,6},{14,10},{7,3},{... | collective-permute-start | bytes 1179656 | tf_op jit(solution)/shard_map/while/body/eval_jaxpr/ppermute | solution.py:27
  250.1 5.7 %collective-permute-start.13 = (f32[2,8,1,256]{3,1,2,0:T(8,128)S(1)}, f32[2,8,1,256]{3,1,2,0:T(8,128)S(1)}, u32[]{:S(2)}, u32[]{:S(2)}) collective-permute-start(f32[2,8,1,256]{3,1,2,0:T(8,128)S(1)} %get-tuple-element.367), channel_id=1, source_target_pairs={{0,1},{1,2},{2,3},{4,5},{5,6},{6,7},{8,9},{9,10},{10,11},{12,13},{... | collective-permute-start | bytes 49160 | tf_op jit(solution)/shard_map/ppermute | solution.py:18
  260.8 5.7 %collective-permute-start.15 = (f32[2,8,1,256]{3,1,2,0:T(8,128)S(1)}, f32[2,8,1,256]{3,1,2,0:T(8,128)S(1)}, u32[]{:S(2)}, u32[]{:S(2)}) collective-permute-start(f32[2,8,1,256]{3,1,2,0:T(8,128)S(1)} %get-tuple-element.365), channel_id=1, source_target_pairs={{0,1},{1,2},{2,3},{4,5},{5,6},{6,7},{8,9},{9,10},{10,11},{12,13},{... | collective-permute-start | bytes 49160 | tf_op jit(solution)/shard_map/ppermute | solution.py:18
  284.3 6.4 %collective-permute-start.19 = (f32[2,8,1,256]{3,1,2,0:T(8,128)S(1)}, f32[2,8,1,256]{3,1,2,0:T(8,128)S(1)}, u32[]{:S(2)}, u32[]{:S(2)}) collective-permute-start(f32[2,8,1,256]{3,1,2,0:T(8,128)S(1)} %get-tuple-element.361), channel_id=1, source_target_pairs={{0,1},{1,2},{2,3},{4,5},{5,6},{6,7},{8,9},{9,10},{10,11},{12,13},{... | collective-permute-start | bytes 49160 | tf_op jit(solution)/shard_map/ppermute | solution.py:18
  (69 other events, 292.7 us)
Sparse Core Ops, SparseCore 0:
  312.4 35.3 all-reduce.1
where the time goes:
time: 359 us; the launch traced here: 356 us
  starting transfers between devices  140 us (39%)
  waiting for transfers between devices  88.5 us (25%)
  local copies, waits for them, and re-layouts  51.5 us (14%)
  other arithmetic  50.6 us (14%)
  between operations  14.9 us (4%)
  matrix products  8.32 us (2%)
    ppermute x24, starting transfers between devices, with_halo(): before = lax.ppermute(last, axis, up)  105 us
    psum x1, waiting for transfers between devices, per_device(): total_bias = lax.psum(bias, 'win')  34.5 us
    ppermute x3, waiting for transfers between devices, passed_along(): lax.ppermute(value, axis, [(source, source + steps) for source in range(i...  33.5 us
    ppermute x24, starting transfers between devices, with_halo(): after = lax.ppermute(initial, axis, down)  31 us
    scatter-add x8, other arithmetic, add_obs(): layer_a.reshape(layer_a.shape[0], -1).at[:, cells].add(values[None, :])  23.2 us
    ppermute x24, waiting for transfers between devices, with_halo(): before = lax.ppermute(last, axis, up)  10.4 us
    ppermute x24, waiting for transfers between devices, with_halo(): after = lax.ppermute(initial, axis, down)  10 us
    dot_general x24, matrix products, tendency(): jnp.einsum('kl,krc->lrc', mix, dxp + dyq, precision=lax.Precision.HIGHEST)  8.32 us
  transfers between devices with their start and end apart: 52, of which 25 were waited for; matrix products, arithmetic and copies ran while one was open for 3% of the time, Pallas kernels for 0%

commit v1 on v0

--- a/solution.py
+++ b/solution.py
@@ -94,7 +94,13 @@
 
     incoming = lax.fori_loop(0, rounds, relay_round, zero_state)
     lam, bias = integrate(incoming)
-    total_bias = lax.psum(bias, "win")
+
+    def touch_limits(body):
+        p_next = jax.lax.all_gather(body, axis_name="win")
+        far_arr = jnp.sum(p_next, 0)
+        return far_arr
+
+    total_bias = touch_limits(bias)
     return (lam[None], total_bias)
 
 

time: 359 us -> 326 us (0.908)
  waiting for transfers between devices: 88.5 us -> 54 us
  blocking collectives: 0 us -> 15.9 us
  between operations: 14.9 us -> 1.51 us
    psum x1 -> x0, waiting for transfers between devices: 34.5 us -> none  [per_device(): total_bias = lax.psum(bias, 'win')]
    all_gather x0 -> x1, blocking collectives: none -> 15.9 us  [touch_limits(): p_next = jax.lax.all_gather(body, axis_name='win')]
  transfers between devices with their start and end apart: 52 -> 51, of which waited for: 25 -> 24; matrix products, arithmetic and copies ran while one was open for 3% -> 3% of each run, Pallas kernels for 0% -> 0%
where the time goes in v1:
time: 326 us; the launch traced here: 323 us
  starting transfers between devices  140 us (43%)
  waiting for transfers between devices  54 us (17%)
  other arithmetic  50.7 us (16%)
  local copies, waits for them, and re-layouts  50.2 us (15%)
  blocking collectives  15.9 us (5%)
  matrix products  8.31 us (3%)
    ppermute x24, starting transfers between devices, with_halo(): before = lax.ppermute(last, axis, up)  105 us
    ppermute x3, waiting for transfers between devices, passed_along(): lax.ppermute(value, axis, [(source, source + steps) for source in range(i...  33.5 us
    ppermute x24, starting transfers between devices, with_halo(): after = lax.ppermute(initial, axis, down)  31 us
    scatter-add x8, other arithmetic, add_obs(): layer_a.reshape(layer_a.shape[0], -1).at[:, cells].add(values[None, :])  23.2 us
    all_gather x1, blocking collectives, touch_limits(): p_next = jax.lax.all_gather(body, axis_name='win')  15.9 us
    ppermute x24, waiting for transfers between devices, with_halo(): before = lax.ppermute(last, axis, up)  10.4 us
    ppermute x24, waiting for transfers between devices, with_halo(): after = lax.ppermute(initial, axis, down)  10 us
    dot_general x24, matrix products, tendency(): jnp.einsum('kl,krc->lrc', mix, dxp + dyq, precision=lax.Precision.HIGHEST)  8.31 us
  transfers between devices with their start and end apart: 51, of which 24 were waited for; matrix products, arithmetic and copies ran while one was open for 3% of the time, Pallas kernels for 0%

profile of v1, /device:TPU:0, one launch (start us, length us, event | category | flops | bytes accessed | tf_op | source)
XLA Modules:
  0.0 323.1 jit_solution(6238025057490587434)
XLA Ops:
  7.0 232.0 %while.17 = (s32[]{:T(128)}, f32[3,8,16,256]{3,1,2,0:T(8,128)S(1)}, s32[1,2,256]{2,1,0:T(2,128)}, f32[1,2,256]{2,1,0:T(2,128)}, f32[16,256]{1,0:T(8,128)S(1)}, /...) while((s32[]{:T(128)}, f32[3,8,16,256]{3,1,2,0:T(8,128)S(1)}, ...), condition=%wide.region_3.4_spmd.clone, body=%wide.region_0.3_spmd.clone.sunk | while | flops 31856224 | bytes 54825772 | solution.py:95
  24.8 4.5 %collective-permute-start.3 = (f32[2,8,1,256]{3,1,2,0:T(8,128)S(1)}, f32[2,8,1,256]{3,1,2,0:T(8,128)S(1)}, u32[]{:S(2)}, u32[]{:S(2)}) collective-permute-start(f32[2,8,1,256]{3,1,2,0:T(8,128)S(1)} %get-tuple-element.612), channel_id=1, source_target_pairs={{0,1},{1,2},{2,3},{4,5},{5,6},{6,7},{8,9},{9,10},{10,11},{12,13},{... | collective-permute-start | bytes 49160 | tf_op jit(solution)/shard_map/while/body/eval_jaxpr/ppermute | solution.py:18
  33.2 4.3 %collective-permute-start.5 = (f32[2,8,1,256]{3,1,2,0:T(8,128)S(1)}, f32[2,8,1,256]{3,1,2,0:T(8,128)S(1)}, u32[]{:S(2)}, u32[]{:S(2)}) collective-permute-start(f32[2,8,1,256]{3,1,2,0:T(8,128)S(1)} %get-tuple-element.628), channel_id=1, source_target_pairs={{0,1},{1,2},{2,3},{4,5},{5,6},{6,7},{8,9},{9,10},{10,11},{12,13},{... | collective-permute-start | bytes 49160 | tf_op jit(solution)/shard_map/while/body/eval_jaxpr/ppermute | solution.py:18
  46.5 4.9 %collective-permute-start.7 = (f32[2,8,1,256]{3,1,2,0:T(8,128)S(1)}, f32[2,8,1,256]{3,1,2,0:T(8,128)S(1)}, u32[]{:S(2)}, u32[]{:S(2)}) collective-permute-start(f32[2,8,1,256]{3,1,2,0:T(8,128)S(1)} %get-tuple-element.646), channel_id=1, source_target_pairs={{0,1},{1,2},{2,3},{4,5},{5,6},{6,7},{8,9},{9,10},{10,11},{12,13},{... | collective-permute-start | bytes 49160 | tf_op jit(solution)/shard_map/while/body/eval_jaxpr/ppermute | solution.py:18
  55.4 4.9 %collective-permute-start.9 = (f32[2,8,1,256]{3,1,2,0:T(8,128)S(1)}, f32[2,8,1,256]{3,1,2,0:T(8,128)S(1)}, u32[]{:S(2)}, u32[]{:S(2)}) collective-permute-start(f32[2,8,1,256]{3,1,2,0:T(8,128)S(1)} %get-tuple-element.662), channel_id=1, source_target_pairs={{0,1},{1,2},{2,3},{4,5},{5,6},{6,7},{8,9},{9,10},{10,11},{12,13},{... | collective-permute-start | bytes 49160 | tf_op jit(solution)/shard_map/while/body/eval_jaxpr/ppermute | solution.py:18
  64.2 4.9 %collective-permute-start.11 = (f32[2,8,1,256]{3,1,2,0:T(8,128)S(1)}, f32[2,8,1,256]{3,1,2,0:T(8,128)S(1)}, u32[]{:S(2)}, u32[]{:S(2)}) collective-permute-start(f32[2,8,1,256]{3,1,2,0:T(8,128)S(1)} %get-tuple-element.678), channel_id=1, source_target_pairs={{0,1},{1,2},{2,3},{4,5},{5,6},{6,7},{8,9},{9,10},{10,11},{12,13},{... | collective-permute-start | bytes 49160 | tf_op jit(solution)/shard_map/while/body/eval_jaxpr/ppermute | solution.py:18
  72.9 11.2 %collective-permute-done.12 = f32[3,8,16,256]{3,1,2,0:T(8,128)S(1)} collective-permute-done((f32[3,8,16,256]{3,1,2,0:T(8,128)S(1)}, f32[3,8,16,256]{3,1,2,0:T(8,128)S(1)}, u32[]{:S(2)}, u32[]{:S(2)}) %collective-permute-start.12) | collective-permute-done | bytes 393248 | tf_op jit(solution)/shard_map/while/body/eval_jaxpr/ppermute | solution.py:27
  92.6 4.4 %collective-permute-start.1 = (f32[2,8,1,256]{3,1,2,0:T(8,128)}, f32[2,8,1,256]{3,1,2,0:T(8,128)}, u32[]{:S(2)}, u32[]{:S(2)}) collective-permute-start(f32[2,8,1,256]{3,1,2,0:T(8,128)} %get-tuple-element.596), channel_id=1, source_target_pairs={{0,1},{1,2},{2,3},{4,5},{5,6},{6,7},{8,9},{9,10},{10,11},{12,13},{... | collective-permute-start | bytes 49160 | tf_op jit(solution)/shard_map/while/body/eval_jaxpr/ppermute | solution.py:18
  102.5 4.3 %collective-permute-start.3 = (f32[2,8,1,256]{3,1,2,0:T(8,128)S(1)}, f32[2,8,1,256]{3,1,2,0:T(8,128)S(1)}, u32[]{:S(2)}, u32[]{:S(2)}) collective-permute-start(f32[2,8,1,256]{3,1,2,0:T(8,128)S(1)} %get-tuple-element.612), channel_id=1, source_target_pairs={{0,1},{1,2},{2,3},{4,5},{5,6},{6,7},{8,9},{9,10},{10,11},{12,13},{... | collective-permute-start | bytes 49160 | tf_op jit(solution)/shard_map/while/body/eval_jaxpr/ppermute | solution.py:18
  110.7 4.3 %collective-permute-start.5 = (f32[2,8,1,256]{3,1,2,0:T(8,128)S(1)}, f32[2,8,1,256]{3,1,2,0:T(8,128)S(1)}, u32[]{:S(2)}, u32[]{:S(2)}) collective-permute-start(f32[2,8,1,256]{3,1,2,0:T(8,128)S(1)} %get-tuple-element.628), channel_id=1, source_target_pairs={{0,1},{1,2},{2,3},{4,5},{5,6},{6,7},{8,9},{9,10},{10,11},{12,13},{... | collective-permute-start | bytes 49160 | tf_op jit(solution)/shard_map/while/body/eval_jaxpr/ppermute | solution.py:18
  124.0 4.9 %collective-permute-start.7 = (f32[2,8,1,256]{3,1,2,0:T(8,128)S(1)}, f32[2,8,1,256]{3,1,2,0:T(8,128)S(1)}, u32[]{:S(2)}, u32[]{:S(2)}) collective-permute-start(f32[2,8,1,256]{3,1,2,0:T(8,128)S(1)} %get-tuple-element.646), channel_id=1, source_target_pairs={{0,1},{1,2},{2,3},{4,5},{5,6},{6,7},{8,9},{9,10},{10,11},{12,13},{... | collective-permute-start | bytes 49160 | tf_op jit(solution)/shard_map/while/body/eval_jaxpr/ppermute | solution.py:18
  132.9 4.9 %collective-permute-start.9 = (f32[2,8,1,256]{3,1,2,0:T(8,128)S(1)}, f32[2,8,1,256]{3,1,2,0:T(8,128)S(1)}, u32[]{:S(2)}, u32[]{:S(2)}) collective-permute-start(f32[2,8,1,256]{3,1,2,0:T(8,128)S(1)} %get-tuple-element.662), channel_id=1, source_target_pairs={{0,1},{1,2},{2,3},{4,5},{5,6},{6,7},{8,9},{9,10},{10,11},{12,13},{... | collective-permute-start | bytes 49160 | tf_op jit(solution)/shard_map/while/body/eval_jaxpr/ppermute | solution.py:18
  141.7 4.9 %collective-permute-start.11 = (f32[2,8,1,256]{3,1,2,0:T(8,128)S(1)}, f32[2,8,1,256]{3,1,2,0:T(8,128)S(1)}, u32[]{:S(2)}, u32[]{:S(2)}) collective-permute-start(f32[2,8,1,256]{3,1,2,0:T(8,128)S(1)} %get-tuple-element.678), channel_id=1, source_target_pairs={{0,1},{1,2},{2,3},{4,5},{5,6},{6,7},{8,9},{9,10},{10,11},{12,13},{... | collective-permute-start | bytes 49160 | tf_op jit(solution)/shard_map/while/body/eval_jaxpr/ppermute | solution.py:18
  150.4 11.2 %collective-permute-done.12 = f32[3,8,16,256]{3,1,2,0:T(8,128)S(1)} collective-permute-done((f32[3,8,16,256]{3,1,2,0:T(8,128)S(1)}, f32[3,8,16,256]{3,1,2,0:T(8,128)S(1)}, u32[]{:S(2)}, u32[]{:S(2)}) %collective-permute-start.12) | collective-permute-done | bytes 393248 | tf_op jit(solution)/shard_map/while/body/eval_jaxpr/ppermute | solution.py:27
  170.1 4.4 %collective-permute-start.1 = (f32[2,8,1,256]{3,1,2,0:T(8,128)}, f32[2,8,1,256]{3,1,2,0:T(8,128)}, u32[]{:S(2)}, u32[]{:S(2)}) collective-permute-start(f32[2,8,1,256]{3,1,2,0:T(8,128)} %get-tuple-element.596), channel_id=1, source_target_pairs={{0,1},{1,2},{2,3},{4,5},{5,6},{6,7},{8,9},{9,10},{10,11},{12,13},{... | collective-permute-start | bytes 49160 | tf_op jit(solution)/shard_map/while/body/eval_jaxpr/ppermute | solution.py:18
  180.0 4.3 %collective-permute-start.3 = (f32[2,8,1,256]{3,1,2,0:T(8,128)S(1)}, f32[2,8,1,256]{3,1,2,0:T(8,128)S(1)}, u32[]{:S(2)}, u32[]{:S(2)}) collective-permute-start(f32[2,8,1,256]{3,1,2,0:T(8,128)S(1)} %get-tuple-element.612), channel_id=1, source_target_pairs={{0,1},{1,2},{2,3},{4,5},{5,6},{6,7},{8,9},{9,10},{10,11},{12,13},{... | collective-permute-start | bytes 49160 | tf_op jit(solution)/shard_map/while/body/eval_jaxpr/ppermute | solution.py:18
  188.2 4.3 %collective-permute-start.5 = (f32[2,8,1,256]{3,1,2,0:T(8,128)S(1)}, f32[2,8,1,256]{3,1,2,0:T(8,128)S(1)}, u32[]{:S(2)}, u32[]{:S(2)}) collective-permute-start(f32[2,8,1,256]{3,1,2,0:T(8,128)S(1)} %get-tuple-element.628), channel_id=1, source_target_pairs={{0,1},{1,2},{2,3},{4,5},{5,6},{6,7},{8,9},{9,10},{10,11},{12,13},{... | collective-permute-start | bytes 49160 | tf_op jit(solution)/shard_map/while/body/eval_jaxpr/ppermute | solution.py:18
  201.5 4.9 %collective-permute-start.7 = (f32[2,8,1,256]{3,1,2,0:T(8,128)S(1)}, f32[2,8,1,256]{3,1,2,0:T(8,128)S(1)}, u32[]{:S(2)}, u32[]{:S(2)}) collective-permute-start(f32[2,8,1,256]{3,1,2,0:T(8,128)S(1)} %get-tuple-element.646), channel_id=1, source_target_pairs={{0,1},{1,2},{2,3},{4,5},{5,6},{6,7},{8,9},{9,10},{10,11},{12,13},{... | collective-permute-start | bytes 49160 | tf_op jit(solution)/shard_map/while/body/eval_jaxpr/ppermute | solution.py:18
  210.4 4.9 %collective-permute-start.9 = (f32[2,8,1,256]{3,1,2,0:T(8,128)S(1)}, f32[2,8,1,256]{3,1,2,0:T(8,128)S(1)}, u32[]{:S(2)}, u32[]{:S(2)}) collective-permute-start(f32[2,8,1,256]{3,1,2,0:T(8,128)S(1)} %get-tuple-element.662), channel_id=1, source_target_pairs={{0,1},{1,2},{2,3},{4,5},{5,6},{6,7},{8,9},{9,10},{10,11},{12,13},{... | collective-permute-start | bytes 49160 | tf_op jit(solution)/shard_map/while/body/eval_jaxpr/ppermute | solution.py:18
  219.1 4.9 %collective-permute-start.11 = (f32[2,8,1,256]{3,1,2,0:T(8,128)S(1)}, f32[2,8,1,256]{3,1,2,0:T(8,128)S(1)}, u32[]{:S(2)}, u32[]{:S(2)}) collective-permute-start(f32[2,8,1,256]{3,1,2,0:T(8,128)S(1)} %get-tuple-element.678), channel_id=1, source_target_pairs={{0,1},{1,2},{2,3},{4,5},{5,6},{6,7},{8,9},{9,10},{10,11},{12,13},{... | collective-permute-start | bytes 49160 | tf_op jit(solution)/shard_map/while/body/eval_jaxpr/ppermute | solution.py:18
  227.9 11.2 %collective-permute-done.12 = f32[3,8,16,256]{3,1,2,0:T(8,128)S(1)} collective-permute-done((f32[3,8,16,256]{3,1,2,0:T(8,128)S(1)}, f32[3,8,16,256]{3,1,2,0:T(8,128)S(1)}, u32[]{:S(2)}, u32[]{:S(2)}) %collective-permute-start.12) | collective-permute-done | bytes 393248 | tf_op jit(solution)/shard_map/while/body/eval_jaxpr/ppermute | solution.py:27
  254.2 4.4 %collective-permute-start.15 = (f32[2,8,1,256]{3,1,2,0:T(8,128)S(1)}, f32[2,8,1,256]{3,1,2,0:T(8,128)S(1)}, u32[]{:S(2)}, u32[]{:S(2)}) collective-permute-start(f32[2,8,1,256]{3,1,2,0:T(8,128)S(1)} %get-tuple-element.376), channel_id=1, source_target_pairs={{0,1},{1,2},{2,3},{4,5},{5,6},{6,7},{8,9},{9,10},{10,11},{12,13},{... | collective-permute-start | bytes 49160 | tf_op jit(solution)/shard_map/ppermute | solution.py:18
  263.4 3.9 %collective-permute-start.17 = (f32[2,8,1,256]{3,1,2,0:T(8,128)S(1)}, f32[2,8,1,256]{3,1,2,0:T(8,128)S(1)}, u32[]{:S(2)}, u32[]{:S(2)}) collective-permute-start(f32[2,8,1,256]{3,1,2,0:T(8,128)S(1)} %get-tuple-element.374), channel_id=1, source_target_pairs={{0,1},{1,2},{2,3},{4,5},{5,6},{6,7},{8,9},{9,10},{10,11},{12,13},{... | collective-permute-start | bytes 49160 | tf_op jit(solution)/shard_map/ppermute | solution.py:18
  305.6 15.9 %all_gather.4 = f32[4,8,16,256]{3,2,1,0:T(8,128)S(1)} all-gather(f32[1,8,16,256]{3,2,1,0:T(8,128)S(1)} %copy.228), channel_id=1, replica_groups=mesh['groups'=2,'win'=4,'lat'=4] {'win'}, dimensions={0}, use_global_device_ids=true | all-gather | bytes 655360 | tf_op jit(solution)/shard_map/all_gather | solution.py:99
  (616 shorter events, 183.0 us)
Async XLA Ops:
  14.3 6.6 %collective-permute-start = (f32[2,8,1,256]{3,1,2,0:T(8,128)}, f32[2,8,1,256]{3,1,2,0:T(8,128)}, u32[]{:S(2)}, u32[]{:S(2)}) collective-permute-start(f32[2,8,1,256]{3,1,2,0:T(8,128)} %get-tuple-element.595), channel_id=1, source_target_pairs={{1,0},{2,1},{3,2},{5,4},{6,5},{7,6},{9,8},{10,9},{11,10},{13,12},{... | collective-permute-start | bytes 49160 | tf_op jit(solution)/shard_map/while/body/eval_jaxpr/ppermute | solution.py:19
  23.5 5.8 %collective-permute-start.2 = (f32[2,8,1,256]{3,1,2,0:T(8,128)S(1)}, f32[2,8,1,256]{3,1,2,0:T(8,128)S(1)}, u32[]{:S(2)}, u32[]{:S(2)}) collective-permute-start(f32[2,8,1,256]{3,1,2,0:T(8,128)S(1)} %get-tuple-element.611), channel_id=1, source_target_pairs={{1,0},{2,1},{3,2},{5,4},{6,5},{7,6},{9,8},{10,9},{11,10},{13,12},{... | collective-permute-start | bytes 49160 | tf_op jit(solution)/shard_map/while/body/eval_jaxpr/ppermute | solution.py:19
  45.2 6.8 %collective-permute-start.6 = (f32[2,8,1,256]{3,1,2,0:T(8,128)S(1)}, f32[2,8,1,256]{3,1,2,0:T(8,128)S(1)}, u32[]{:S(2)}, u32[]{:S(2)}) collective-permute-start(f32[2,8,1,256]{3,1,2,0:T(8,128)S(1)} %get-tuple-element.645), channel_id=1, source_target_pairs={{1,0},{2,1},{3,2},{5,4},{6,5},{7,6},{9,8},{10,9},{11,10},{13,12},{... | collective-permute-start | bytes 49160 | tf_op jit(solution)/shard_map/while/body/eval_jaxpr/ppermute | solution.py:19
  54.1 6.2 %collective-permute-start.8 = (f32[2,8,1,256]{3,1,2,0:T(8,128)S(1)}, f32[2,8,1,256]{3,1,2,0:T(8,128)S(1)}, u32[]{:S(2)}, u32[]{:S(2)}) collective-permute-start(f32[2,8,1,256]{3,1,2,0:T(8,128)S(1)} %get-tuple-element.661), channel_id=1, source_target_pairs={{1,0},{2,1},{3,2},{5,4},{6,5},{7,6},{9,8},{10,9},{11,10},{13,12},{... | collective-permute-start | bytes 49160 | tf_op jit(solution)/shard_map/while/body/eval_jaxpr/ppermute | solution.py:19
  55.4 5.7 %collective-permute-start.9 = (f32[2,8,1,256]{3,1,2,0:T(8,128)S(1)}, f32[2,8,1,256]{3,1,2,0:T(8,128)S(1)}, u32[]{:S(2)}, u32[]{:S(2)}) collective-permute-start(f32[2,8,1,256]{3,1,2,0:T(8,128)S(1)} %get-tuple-element.662), channel_id=1, source_target_pairs={{0,1},{1,2},{2,3},{4,5},{5,6},{6,7},{8,9},{9,10},{10,11},{12,13},{... | collective-permute-start | bytes 49160 | tf_op jit(solution)/shard_map/while/body/eval_jaxpr/ppermute | solution.py:18
  62.9 6.2 %collective-permute-start.10 = (f32[2,8,1,256]{3,1,2,0:T(8,128)S(1)}, f32[2,8,1,256]{3,1,2,0:T(8,128)S(1)}, u32[]{:S(2)}, u32[]{:S(2)}) collective-permute-start(f32[2,8,1,256]{3,1,2,0:T(8,128)S(1)} %get-tuple-element.677), channel_id=1, source_target_pairs={{1,0},{2,1},{3,2},{5,4},{6,5},{7,6},{9,8},{10,9},{11,10},{13,12},{... | collective-permute-start | bytes 49160 | tf_op jit(solution)/shard_map/while/body/eval_jaxpr/ppermute | solution.py:19
  64.2 5.7 %collective-permute-start.11 = (f32[2,8,1,256]{3,1,2,0:T(8,128)S(1)}, f32[2,8,1,256]{3,1,2,0:T(8,128)S(1)}, u32[]{:S(2)}, u32[]{:S(2)}) collective-permute-start(f32[2,8,1,256]{3,1,2,0:T(8,128)S(1)} %get-tuple-element.678), channel_id=1, source_target_pairs={{0,1},{1,2},{2,3},{4,5},{5,6},{6,7},{8,9},{9,10},{10,11},{12,13},{... | collective-permute-start | bytes 49160 | tf_op jit(solution)/shard_map/while/body/eval_jaxpr/ppermute | solution.py:18
  71.6 12.5 %collective-permute-start.12 = (f32[3,8,16,256]{3,1,2,0:T(8,128)S(1)}, f32[3,8,16,256]{3,1,2,0:T(8,128)S(1)}, u32[]{:S(2)}, u32[]{:S(2)}) collective-permute-start(f32[3,8,16,256]{3,1,2,0:T(8,128)S(1)} %fusion.479), channel_id=1, source_target_pairs={{4,0},{8,4},{12,8},{5,1},{9,5},{13,9},{6,2},{10,6},{14,10},{7,3},{... | collective-permute-start | bytes 1179656 | tf_op jit(solution)/shard_map/while/body/eval_jaxpr/ppermute | solution.py:27
  91.3 7.4 %collective-permute-start = (f32[2,8,1,256]{3,1,2,0:T(8,128)}, f32[2,8,1,256]{3,1,2,0:T(8,128)}, u32[]{:S(2)}, u32[]{:S(2)}) collective-permute-start(f32[2,8,1,256]{3,1,2,0:T(8,128)} %get-tuple-element.595), channel_id=1, source_target_pairs={{1,0},{2,1},{3,2},{5,4},{6,5},{7,6},{9,8},{10,9},{11,10},{13,12},{... | collective-permute-start | bytes 49160 | tf_op jit(solution)/shard_map/while/body/eval_jaxpr/ppermute | solution.py:19
  92.6 6.1 %collective-permute-start.1 = (f32[2,8,1,256]{3,1,2,0:T(8,128)}, f32[2,8,1,256]{3,1,2,0:T(8,128)}, u32[]{:S(2)}, u32[]{:S(2)}) collective-permute-start(f32[2,8,1,256]{3,1,2,0:T(8,128)} %get-tuple-element.596), channel_id=1, source_target_pairs={{0,1},{1,2},{2,3},{4,5},{5,6},{6,7},{8,9},{9,10},{10,11},{12,13},{... | collective-permute-start | bytes 49160 | tf_op jit(solution)/shard_map/while/body/eval_jaxpr/ppermute | solution.py:18
  122.7 6.8 %collective-permute-start.6 = (f32[2,8,1,256]{3,1,2,0:T(8,128)S(1)}, f32[2,8,1,256]{3,1,2,0:T(8,128)S(1)}, u32[]{:S(2)}, u32[]{:S(2)}) collective-permute-start(f32[2,8,1,256]{3,1,2,0:T(8,128)S(1)} %get-tuple-element.645), channel_id=1, source_target_pairs={{1,0},{2,1},{3,2},{5,4},{6,5},{7,6},{9,8},{10,9},{11,10},{13,12},{... | collective-permute-start | bytes 49160 | tf_op jit(solution)/shard_map/while/body/eval_jaxpr/ppermute | solution.py:19
  131.6 6.2 %collective-permute-start.8 = (f32[2,8,1,256]{3,1,2,0:T(8,128)S(1)}, f32[2,8,1,256]{3,1,2,0:T(8,128)S(1)}, u32[]{:S(2)}, u32[]{:S(2)}) collective-permute-start(f32[2,8,1,256]{3,1,2,0:T(8,128)S(1)} %get-tuple-element.661), channel_id=1, source_target_pairs={{1,0},{2,1},{3,2},{5,4},{6,5},{7,6},{9,8},{10,9},{11,10},{13,12},{... | collective-permute-start | bytes 49160 | tf_op jit(solution)/shard_map/while/body/eval_jaxpr/ppermute | solution.py:19
  140.3 6.2 %collective-permute-start.10 = (f32[2,8,1,256]{3,1,2,0:T(8,128)S(1)}, f32[2,8,1,256]{3,1,2,0:T(8,128)S(1)}, u32[]{:S(2)}, u32[]{:S(2)}) collective-permute-start(f32[2,8,1,256]{3,1,2,0:T(8,128)S(1)} %get-tuple-element.677), channel_id=1, source_target_pairs={{1,0},{2,1},{3,2},{5,4},{6,5},{7,6},{9,8},{10,9},{11,10},{13,12},{... | collective-permute-start | bytes 49160 | tf_op jit(solution)/shard_map/while/body/eval_jaxpr/ppermute | solution.py:19
  149.1 12.5 %collective-permute-start.12 = (f32[3,8,16,256]{3,1,2,0:T(8,128)S(1)}, f32[3,8,16,256]{3,1,2,0:T(8,128)S(1)}, u32[]{:S(2)}, u32[]{:S(2)}) collective-permute-start(f32[3,8,16,256]{3,1,2,0:T(8,128)S(1)} %fusion.479), channel_id=1, source_target_pairs={{4,0},{8,4},{12,8},{5,1},{9,5},{13,9},{6,2},{10,6},{14,10},{7,3},{... | collective-permute-start | bytes 1179656 | tf_op jit(solution)/shard_map/while/body/eval_jaxpr/ppermute | solution.py:27
  168.8 7.4 %collective-permute-start = (f32[2,8,1,256]{3,1,2,0:T(8,128)}, f32[2,8,1,256]{3,1,2,0:T(8,128)}, u32[]{:S(2)}, u32[]{:S(2)}) collective-permute-start(f32[2,8,1,256]{3,1,2,0:T(8,128)} %get-tuple-element.595), channel_id=1, source_target_pairs={{1,0},{2,1},{3,2},{5,4},{6,5},{7,6},{9,8},{10,9},{11,10},{13,12},{... | collective-permute-start | bytes 49160 | tf_op jit(solution)/shard_map/while/body/eval_jaxpr/ppermute | solution.py:19
  170.1 6.1 %collective-permute-start.1 = (f32[2,8,1,256]{3,1,2,0:T(8,128)}, f32[2,8,1,256]{3,1,2,0:T(8,128)}, u32[]{:S(2)}, u32[]{:S(2)}) collective-permute-start(f32[2,8,1,256]{3,1,2,0:T(8,128)} %get-tuple-element.596), channel_id=1, source_target_pairs={{0,1},{1,2},{2,3},{4,5},{5,6},{6,7},{8,9},{9,10},{10,11},{12,13},{... | collective-permute-start | bytes 49160 | tf_op jit(solution)/shard_map/while/body/eval_jaxpr/ppermute | solution.py:18
  200.2 6.8 %collective-permute-start.6 = (f32[2,8,1,256]{3,1,2,0:T(8,128)S(1)}, f32[2,8,1,256]{3,1,2,0:T(8,128)S(1)}, u32[]{:S(2)}, u32[]{:S(2)}) collective-permute-start(f32[2,8,1,256]{3,1,2,0:T(8,128)S(1)} %get-tuple-element.645), channel_id=1, source_target_pairs={{1,0},{2,1},{3,2},{5,4},{6,5},{7,6},{9,8},{10,9},{11,10},{13,12},{... | collective-permute-start | bytes 49160 | tf_op jit(solution)/shard_map/while/body/eval_jaxpr/ppermute | solution.py:19
  201.5 5.7 %collective-permute-start.7 = (f32[2,8,1,256]{3,1,2,0:T(8,128)S(1)}, f32[2,8,1,256]{3,1,2,0:T(8,128)S(1)}, u32[]{:S(2)}, u32[]{:S(2)}) collective-permute-start(f32[2,8,1,256]{3,1,2,0:T(8,128)S(1)} %get-tuple-element.646), channel_id=1, source_target_pairs={{0,1},{1,2},{2,3},{4,5},{5,6},{6,7},{8,9},{9,10},{10,11},{12,13},{... | collective-permute-start | bytes 49160 | tf_op jit(solution)/shard_map/while/body/eval_jaxpr/ppermute | solution.py:18
  209.1 6.2 %collective-permute-start.8 = (f32[2,8,1,256]{3,1,2,0:T(8,128)S(1)}, f32[2,8,1,256]{3,1,2,0:T(8,128)S(1)}, u32[]{:S(2)}, u32[]{:S(2)}) collective-permute-start(f32[2,8,1,256]{3,1,2,0:T(8,128)S(1)} %get-tuple-element.661), channel_id=1, source_target_pairs={{1,0},{2,1},{3,2},{5,4},{6,5},{7,6},{9,8},{10,9},{11,10},{13,12},{... | collective-permute-start | bytes 49160 | tf_op jit(solution)/shard_map/while/body/eval_jaxpr/ppermute | solution.py:19
  217.8 6.2 %collective-permute-start.10 = (f32[2,8,1,256]{3,1,2,0:T(8,128)S(1)}, f32[2,8,1,256]{3,1,2,0:T(8,128)S(1)}, u32[]{:S(2)}, u32[]{:S(2)}) collective-permute-start(f32[2,8,1,256]{3,1,2,0:T(8,128)S(1)} %get-tuple-element.677), channel_id=1, source_target_pairs={{1,0},{2,1},{3,2},{5,4},{6,5},{7,6},{9,8},{10,9},{11,10},{13,12},{... | collective-permute-start | bytes 49160 | tf_op jit(solution)/shard_map/while/body/eval_jaxpr/ppermute | solution.py:19
  226.6 12.5 %collective-permute-start.12 = (f32[3,8,16,256]{3,1,2,0:T(8,128)S(1)}, f32[3,8,16,256]{3,1,2,0:T(8,128)S(1)}, u32[]{:S(2)}, u32[]{:S(2)}) collective-permute-start(f32[3,8,16,256]{3,1,2,0:T(8,128)S(1)} %fusion.479), channel_id=1, source_target_pairs={{4,0},{8,4},{12,8},{5,1},{9,5},{13,9},{6,2},{10,6},{14,10},{7,3},{... | collective-permute-start | bytes 1179656 | tf_op jit(solution)/shard_map/while/body/eval_jaxpr/ppermute | solution.py:27
  243.5 5.7 %collective-permute-start.13 = (f32[2,8,1,256]{3,1,2,0:T(8,128)S(1)}, f32[2,8,1,256]{3,1,2,0:T(8,128)S(1)}, u32[]{:S(2)}, u32[]{:S(2)}) collective-permute-start(f32[2,8,1,256]{3,1,2,0:T(8,128)S(1)} %get-tuple-element.378), channel_id=1, source_target_pairs={{0,1},{1,2},{2,3},{4,5},{5,6},{6,7},{8,9},{9,10},{10,11},{12,13},{... | collective-permute-start | bytes 49160 | tf_op jit(solution)/shard_map/ppermute | solution.py:18
  254.2 5.7 %collective-permute-start.15 = (f32[2,8,1,256]{3,1,2,0:T(8,128)S(1)}, f32[2,8,1,256]{3,1,2,0:T(8,128)S(1)}, u32[]{:S(2)}, u32[]{:S(2)}) collective-permute-start(f32[2,8,1,256]{3,1,2,0:T(8,128)S(1)} %get-tuple-element.376), channel_id=1, source_target_pairs={{0,1},{1,2},{2,3},{4,5},{5,6},{6,7},{8,9},{9,10},{10,11},{12,13},{... | collective-permute-start | bytes 49160 | tf_op jit(solution)/shard_map/ppermute | solution.py:18
  277.7 6.4 %collective-permute-start.19 = (f32[2,8,1,256]{3,1,2,0:T(8,128)S(1)}, f32[2,8,1,256]{3,1,2,0:T(8,128)S(1)}, u32[]{:S(2)}, u32[]{:S(2)}) collective-permute-start(f32[2,8,1,256]{3,1,2,0:T(8,128)S(1)} %get-tuple-element.372), channel_id=1, source_target_pairs={{0,1},{1,2},{2,3},{4,5},{5,6},{6,7},{8,9},{9,10},{10,11},{12,13},{... | collective-permute-start | bytes 49160 | tf_op jit(solution)/shard_map/ppermute | solution.py:18
  (68 other events, 286.9 us)
